TPU v7x, 128 devices: a whole 4x4x4 slice. The times are simulated.
128 devices in a mesh: row: 8 (over z_lo, y), col: 16 (over z_hi, x, core).
Axes of the slice: x: 4, y: 4, z: 4 (z_hi: 2, z_lo: 2; z = z_hi * 2 + z_lo), core: 2. Of those that a mesh axis runs over, the one named last changes fastest.
Arguments:
- observed: float32 [4, 65536], P(None, ('row', 'col')), may hold values from -50 to 50
- tile_values: bfloat16 [256, 32, 256, 256], P('row', 'col'), may hold values from -2.2649514 to 2.2649514
- tile_cols: int32 [256, 32], P('row', 'col'), may hold values from 0 to 255
Outputs:
- solution: float32 [4, 1048576], P(None, ('col', 'row'))
- residual_ratio: float32 [4], replicated
All inputs are finite; a program needn't handle non-finite values.
Results may differ from a plain program's by a relative error of at most 0.0021.
Values may be sent and summed in bfloat16 or wider, within the bound.
A program may use at most 128 MiB of HBM per device.

v0:
```python
import jax
import jax.numpy as jnp
from jax import lax
from jax.sharding import PartitionSpec as P

ITERS = 2
N = 1048576


epsilon_sq = 1e-06


def local(observed, tile_values, tile_cols):
    right_sides = observed.shape[0]
    row_tiles = tile_values.shape[0]
    per_block = tile_values.shape[1]
    tile_size = tile_values.shape[2]
    col_tiles = N // (tile_size * lax.axis_size("col"))
    panel_len = col_tiles * tile_size
    share_len = panel_len // lax.axis_size("row")
    flat_cols = tile_cols.reshape(-1)

    def adjoint_map(left_bf):
        gathered = lax.all_gather(left_bf, "col", axis=1, tiled=True).reshape(
            right_sides, row_tiles, tile_size
        )
        tile_terms = jnp.einsum(
            "rktj,nrt->nrkj", tile_values, gathered, preferred_element_type=jnp.float32
        )
        tile_terms = tile_terms.reshape(right_sides, row_tiles * per_block, tile_size)
        placed = (
            jnp.zeros((right_sides, col_tiles, tile_size), jnp.float32)
            .at[:, flat_cols]
            .add(tile_terms)
        )
        placed = placed.reshape(right_sides, panel_len)
        summed = lax.psum_scatter(placed, "row", scatter_dimension=1, tiled=True)
        return summed

    def lanczos_pair(left_raw, right_vec):
        beta_sq = lax.psum(jnp.sum(left_raw * left_raw, axis=1), ("row", "col"))
        beta_norm = jnp.sqrt(beta_sq + epsilon_sq)
        product = adjoint_map(left_raw.astype(jnp.bfloat16))
        right_raw = product / beta_norm[:, None] - beta_norm[:, None] * right_vec
        alpha_sq = lax.psum(jnp.sum(right_raw * right_raw, axis=1), ("row", "col"))
        alpha_norm = jnp.sqrt(alpha_sq + epsilon_sq)
        return (beta_norm, alpha_norm, right_raw)

    blank_right = jnp.zeros((right_sides, share_len), jnp.float32)
    beta_norm, alpha_norm, right_raw = lanczos_pair(observed, blank_right)
    first_beta = beta_norm
    left_vec = observed / beta_norm[:, None]
    right_vec = right_raw / alpha_norm[:, None]
    right_bf = right_raw.astype(jnp.bfloat16)
    phibar = beta_norm
    rhobar = alpha_norm
    direction = right_vec
    solution = jnp.zeros_like(right_vec)
    for iteration in range(ITERS):
        whole_panel = lax.all_gather(right_bf, "row", axis=1, tiled=True)
        picked = jnp.take(whole_panel.reshape(right_sides, col_tiles, tile_size), tile_cols, axis=1)
        partial_rows = jnp.einsum(
            "rktj,nrkj->nrt", tile_values, picked, preferred_element_type=jnp.float32
        )
        left_raw = (
            lax.psum_scatter(
                partial_rows.reshape(right_sides, row_tiles * tile_size),
                "col",
                scatter_dimension=1,
                tiled=True,
            )
            / alpha_norm[:, None]
            - alpha_norm[:, None] * left_vec
        )
        beta_norm, alpha_norm, right_raw = lanczos_pair(left_raw, right_vec)
        left_vec = left_raw / beta_norm[:, None]
        right_vec = right_raw / alpha_norm[:, None]
        right_bf = right_raw.astype(jnp.bfloat16)
        rho_val = jnp.sqrt(rhobar * rhobar + beta_norm * beta_norm)
        cosine = rhobar / rho_val
        sine_val = beta_norm / rho_val
        theta_val = sine_val * alpha_norm
        rhobar = -cosine * alpha_norm
        phi_val = cosine * phibar
        phibar = sine_val * phibar
        solution = solution + (phi_val / rho_val)[:, None] * direction
        direction = right_vec - (theta_val / rho_val)[:, None] * direction
    return (solution, phibar / first_beta)


def solution(mesh):
    in_specs = (P(None, ("row", "col")), P("row", "col", None, None), P("row", "col"))
    out_specs = (P(None, ("col", "row")), P())
    return jax.shard_map(local, mesh=mesh, in_specs=in_specs, out_specs=out_specs, check_vma=False)
```

profile of v0, /device:TPU:1, one launch (start us, length us, event | category | flops | bytes accessed | tf_op | source)
XLA Modules:
  0.0 1160.2 jit_solution(9524676217768432283)
XLA Ops:
  7.2 0.0 reduce-scatter.13.cloned.1.call-start
  7.2 0.9 fusion.20
  8.1 26.5 %all_gather.12 = bf16[4,8192]{1,0:T(4,128)(2,1)S(1)} all-gather(bf16[4,512]{1,0:T(4,128)(2,1)S(1)} %get-tuple-element.13), channel_id=1, replica_groups=mesh['row'=8,'col'=16] {'col'}, dimensions={1}, use_global_device_ids=true | all-gather | bytes 69632 | tf_op jit(solution)/shard_map/all_gather | solution.py:24
  34.6 0.8 copy.17
  35.4 0.1 reshape.77
  35.5 4.6 fusion.21
  40.0 0.1 broadcast.38.clone
  40.2 2.8 scatter_fusion
  43.0 16.1 %copy.26 = f32[4,65536]{0,1:T(8,128)} copy(f32[4,65536]{1,0:T(4,128)S(1)} %bitcast.65) | data formatting | bytes 2097152
  59.1 0.0 reduce-scatter.15.cloned.1.call-start
  59.2 369.9 %psum.35 = f32[4]{0:T(128)S(1)} all-reduce(f32[4]{0:T(128)S(1)} %get-tuple-element.14), channel_id=1, replica_groups=mesh['row'=8,'col'=16] {'row','col'}, use_global_device_ids=true, to_apply=%region_3.0 | all-reduce | flops 4 | bytes 32 | tf_op jit(solution)/shard_map/psum | solution.py:41
  429.1 0.1 copy.19
  429.2 0.1 reshape.124
  429.3 0.1 copy.18
  429.4 0.0 reduce-scatter.13.cloned.1.call-done
  429.5 2.8 copy.27
  432.3 0.3 multiply_reduce_fusion.1
  432.6 22.8 %all_gather.13 = bf16[4,65536]{1,0:T(4,128)(2,1)S(1)} all-gather(bf16[4,8192]{1,0:T(4,128)(2,1)S(1)} %convert_element_type.13), channel_id=1, replica_groups=mesh['row'=8,'col'=16] {'row'}, dimensions={1}, use_global_device_ids=true | all-gather | bytes 589824 | tf_op jit(solution)/shard_map/all_gather | solution.py:60
  455.4 0.7 gather_fusion
  456.2 5.7 fusion.2
  461.8 2.6 copy.28
  464.5 0.0 reduce-scatter.17.cloned.1.call-start
  464.5 74.8 %psum.36 = f32[4]{0:T(128)S(1)} all-reduce(f32[4]{0:T(128)S(1)} %get-tuple-element.11), channel_id=1, replica_groups=mesh['row'=8,'col'=16] {'row','col'}, use_global_device_ids=true, to_apply=%region_5.0 | all-reduce | flops 4 | bytes 32 | tf_op jit(solution)/shard_map/psum | solution.py:45
  539.3 8.1 reduce-scatter.15.cloned.1.call-done
  547.4 1.1 copy.29
  548.5 0.2 multiply_reduce_fusion.2
  548.7 23.2 %all_gather.14 = bf16[4,8192]{1,0:T(4,128)(2,1)S(1)} all-gather(bf16[4,512]{1,0:T(4,128)(2,1)S(1)} %convert_element_type.14), channel_id=1, replica_groups=mesh['row'=8,'col'=16] {'col'}, dimensions={1}, use_global_device_ids=true | all-gather | bytes 69632 | tf_op jit(solution)/shard_map/all_gather | solution.py:24
  571.9 4.6 fusion.22
  576.4 0.1 broadcast.38
  576.6 2.8 scatter_fusion.1
  579.4 16.1 %copy.30 = f32[4,65536]{0,1:T(8,128)} copy(f32[4,65536]{1,0:T(4,128)S(1)} %bitcast.64) | data formatting | bytes 2097152
  595.5 0.0 reduce-scatter.19.cloned.1.call-start
  595.6 371.7 %psum.37 = f32[4]{0:T(128)S(1)} all-reduce(f32[4]{0:T(128)S(1)} %get-tuple-element.9), channel_id=1, replica_groups=mesh['row'=8,'col'=16] {'row','col'}, use_global_device_ids=true, to_apply=%region_8.10 | all-reduce | flops 4 | bytes 32 | tf_op jit(solution)/shard_map/psum | solution.py:41
  967.3 2.8 copy.31
  970.2 0.1 fusion.19
  970.3 23.0 %all_gather.15 = bf16[4,65536]{1,0:T(4,128)(2,1)S(1)} all-gather(bf16[4,8192]{1,0:T(4,128)(2,1)S(1)} %get-tuple-element.7), channel_id=1, replica_groups=mesh['row'=8,'col'=16] {'row'}, dimensions={1}, use_global_device_ids=true | all-gather | bytes 589824 | tf_op jit(solution)/shard_map/all_gather | solution.py:60
  993.3 0.7 gather_fusion.1
  994.0 5.7 fusion
  999.7 2.6 copy.32
  1002.3 0.2 multiply_reduce_fusion
  1002.5 0.0 reduce-scatter.19.cloned.1.call-update
  1002.5 74.9 %psum.38 = f32[4]{0:T(128)S(1)} all-reduce(f32[4]{0:T(128)S(1)} %multiply_reduce_fusion), channel_id=1, replica_groups=mesh['row'=8,'col'=16] {'row','col'}, use_global_device_ids=true, to_apply=%region_12.14 | all-reduce | flops 4 | bytes 32 | tf_op jit(solution)/shard_map/psum | solution.py:45
  1077.4 8.0 reduce-scatter.19.cloned.1.call-done
  1085.5 1.1 copy.33
  1086.5 0.2 fusion.11
  1086.7 65.6 %psum.39 = f32[4]{0:T(128)S(1)} all-reduce(f32[4]{0:T(128)S(1)} %fusion.11), channel_id=1, replica_groups=mesh['row'=8,'col'=16] {'row','col'}, use_global_device_ids=true, to_apply=%region_15.17 | all-reduce | flops 4 | bytes 32 | tf_op jit(solution)/shard_map/psum | solution.py:41
  1152.3 0.6 multiply_divide_fusion
  1152.9 0.8 multiply_add_fusion
  (19 shorter events, 0.2 us)
Async XLA Ops:
  7.2 422.3 %reduce-scatter.13.cloned.1.call-start = ((), (), s32[]{:S(2)}) async-start(), calls=%async_computation.4 | async-start | bytes 37748736
  59.1 370.0 %copy-start.1 = (s32[32,2]{0,1:T(2,128)S(1)}, s32[32,2]{0,1:T(2,128)}, u32[]{:S(2)}) copy-start(s32[32,2]{0,1:T(2,128)} %param.7) | copy-start | bytes 772
  59.1 488.3 %reduce-scatter.15.cloned.1.call-start = ((), (), s32[]{:S(2)}) async-start(), calls=%async_computation.5 | async-start | bytes 4456448
  456.1 92.3 %copy-start = (f32[4,512]{1,0:T(4,128)S(1)}, f32[4,512]{1,0:T(4,128)}, u32[]{:S(2)}) copy-start(f32[4,512]{1,0:T(4,128)} %param.5) | copy-start | bytes 24580
  464.5 502.9 %reduce-scatter.17.cloned.1.call-start = ((), (), s32[]{:S(2)}) async-start(), calls=%async_computation.6 | async-start | bytes 37748736
  595.5 489.9 %reduce-scatter.19.cloned.1.call-start = ((), (), s32[]{:S(2)}) async-start(), calls=%async_computation.7 | async-start | bytes 4456448
Sparse Core Ops, SparseCore 0:
  59.3 325.6 reduce-scatter.12
  464.6 82.7 reduce-scatter.14
  595.7 327.5 reduce-scatter.16
  1002.7 82.7 reduce-scatter.18
where the time goes:
time: 1160 us
  blocking collectives  1050 us (91%)
  local copies, waits for them, and re-layouts  48 us (4%)
  matrix products  20.5 us (2%)
  waiting for transfers between devices  16.2 us (1%)
  between operations  13.9 us (1%)
    psum x3, blocking collectives, lanczos_pair(): beta_sq = lax.psum(jnp.sum(left_raw * left_raw, axis=1), ('row', 'col'))  807 us
    psum x2, blocking collectives, lanczos_pair(): alpha_sq = lax.psum(jnp.sum(right_raw * right_raw, axis=1), ('row', 'col'))  150 us
    all_gather x2, blocking collectives, adjoint_map(): lax.all_gather(left_bf, 'col', axis=1, tiled=True)  49.7 us
    unnamed x13, local copies, waits for them, and re-layouts  46 us
    all_gather x2, blocking collectives, local(): whole_panel = lax.all_gather(right_bf, 'row', axis=1, tiled=True)  45.8 us
  transfers between devices with their start and end apart: 4, of which 2 were waited for; matrix products, arithmetic and copies ran while one was open for 0% of the time, Pallas kernels for 0%

commit v1 on v0

v1 whole, which is shorter than its diff:
```python
import functools

import jax
import jax.numpy as jnp
from jax import lax
from jax.experimental import pallas as pl
from jax.experimental.pallas import tpu as pltpu
from jax.sharding import PartitionSpec as P

ITERS = 2
N = 1048576

epsilon_sq = 1e-06

MESH = pl.DeviceIdType.MESH
COL_SUM = jnp.float32
LOAD_PARTS = 8
GROUP = 4
HALVES = 2


def scope(name):
    return jax.named_scope(name)


def norm_of(squares):
    total = jnp.sum(squares, axis=1, keepdims=True)
    return jnp.broadcast_to(jnp.sqrt(total + epsilon_sq), squares.shape)


def sum_of_squares(vectors):
    squares = vectors[0] * vectors[0]
    for vector in vectors[1:]:
        squares = squares + vector * vector
    return squares


def offsets(count):
    if count == 16:
        steps = [(z, x, c) for z in range(2) for x in range(4) for c in range(2)]
        return (8, 2, 1), (2, 4, 2), sorted(steps, key=lambda s: (2 * s[0] + min(s[1], 4 - s[1]), s))
    if count == 8:
        steps = [(z, y, 0) for z in range(2) for y in range(4)]
        return (4, 1, 1), (2, 4, 1), sorted(steps, key=lambda s: (s[0], min(s[1], 4 - s[1]), s))
    return (count, 1, 1), (1, count, 1), [(0, d, 0) for d in range(count)]


def peer_list(me, count):
    strides, sizes, steps = offsets(count)
    places = [lax.rem(lax.div(me, stride), size) for stride, size in zip(strides, sizes)]
    peers = []
    for step in steps:
        peer = 0
        for place, size, stride, d in zip(places, sizes, strides, step):
            if size > 1:
                peer = peer + lax.rem(place + d, size) * stride
        peers.append(peer)
    return peers


def solver_kernel(
    rows, cols, rays, own,
    observed_hbm, columns_hbm, tiles_hbm,
    first_ref, second_ref, left_ref, stats_ref,
    observed_ref, cols_ref, cols_vec, tiles, turned, terms, ray_part, left_panel, voxel_panel, voxel_send, voxel_recv, low_send, low_recv,
    ray_send, ray_recv, norm_col, norm_row, table_vec, table_ref,
    input_sem, load_sem, table_sem, lp_send_sem, lp_recv_sem, vs_send_sem, vs_recv_sem, vp_send_sem, vp_recv_sem,
    lo_send_sem, lo_recv_sem, rs_send_sem, rs_recv_sem, nc_send_sem, nc_recv_sem, nr_send_sem, nr_recv_sem,
):
    f32 = jnp.float32
    bf16 = jnp.bfloat16
    me_row = lax.axis_index("row")
    me_col = lax.axis_index("col")
    row_tiles = tiles.shape[0]
    per_block = tiles.shape[1]
    tile_size = tiles.shape[2]
    half = tile_size // HALVES
    sides = observed_ref.shape[0]
    load_rows = row_tiles // LOAD_PARTS
    flat = row_tiles * per_block
    key_rows = table_vec.shape[0] - per_block
    key_lanes = table_vec.shape[1]
    row_peers = peer_list(me_row, rows)
    col_peers = peer_list(me_col, cols)

    def copy_to(axis, peer, src, dst, send_sem, recv_sem):
        return pltpu.make_async_remote_copy(
            src_ref=src, dst_ref=dst, send_sem=send_sem, recv_sem=recv_sem,
            device_id={axis: peer}, device_id_type=MESH,
        )

    def each(me, count, body):
        def step(d, carry):
            body(lax.rem(me + d, count))
            return carry

        lax.fori_loop(1, count, step, 0)

    def tile_loop(count, unroll, body):
        def step(base, carry):
            for j in range(unroll):
                body(base * unroll + j)
            return carry

        lax.fori_loop(0, count // unroll, step, 0)

    def fold(squares):
        return squares[:, :half] + squares[:, half:]

    def split(value):
        high = value.astype(bf16)
        return high, (value - high.astype(f32)).astype(bf16)

    barrier = pltpu.get_barrier_semaphore()
    each(me_col, cols, lambda p: pl.semaphore_signal(barrier, inc=1, device_id={"col": p}, device_id_type=MESH))
    each(me_row, rows, lambda p: pl.semaphore_signal(barrier, inc=1, device_id={"row": p}, device_id_type=MESH))

    def load_part(part):
        piece = pl.ds(part * load_rows, load_rows)
        return pltpu.make_async_copy(tiles_hbm.at[piece], tiles.at[piece], load_sem.at[part])

    loads = (
        pltpu.make_async_copy(observed_hbm, observed_ref, input_sem.at[0]),
        pltpu.make_async_copy(columns_hbm, cols_ref, input_sem.at[1]),
        pltpu.make_async_copy(columns_hbm, cols_vec, input_sem.at[2]),
    )
    for load in loads:
        load.start()
    for part in range(LOAD_PARTS):
        load_part(part).start()

    def side_tile(i):
        return observed_ref[:, i * tile_size:(i + 1) * tile_size]

    def publish_left(turn, vectors):
        for i, vector in enumerate(vectors):
            left_panel[turn, me_col, i] = vector.astype(bf16)
        high, low = split(fold(sum_of_squares(vectors)))
        left_panel[turn, me_col, rays, :, :half] = high
        left_panel[turn, me_col, rays, :, half:] = low

    def left_copy(turn, peer, slot):
        return copy_to(
            "col", peer, left_panel.at[turn, slot], left_panel.at[turn, slot],
            lp_send_sem.at[turn, peer], lp_recv_sem.at[turn, slot],
        )

    def send_left(turn):
        for p in reversed(col_peers[1:]):
            left_copy(turn, p, me_col).start()

    def make_table():
        columns = cols_vec[...]
        numbers = lax.broadcasted_iota(jnp.int32, columns.shape, 0) * row_tiles + lax.broadcasted_iota(
            jnp.int32, columns.shape, 1
        )
        key_shape = (key_rows, key_lanes)
        keys = lax.broadcasted_iota(jnp.int32, key_shape, 0) * key_lanes + lax.broadcasted_iota(jnp.int32, key_shape, 1)
        before = jnp.zeros_like(columns)
        last = jnp.zeros_like(keys)
        for t in range(flat):
            column = cols_ref[t // row_tiles, t % row_tiles]
            before = jnp.where((columns == column) & (numbers > t), t + 1, before)
            last = jnp.where(keys == column, t + 1, last)
        table_vec[...] = jnp.zeros_like(table_vec)
        table_vec[:key_rows, :] = last
        table_vec[key_rows:, :row_tiles] = before
        copy = pltpu.make_async_copy(table_vec, table_ref, table_sem)
        copy.start()
        copy.wait()

    def last_term(c):
        return table_ref[lax.div(c, key_lanes), lax.rem(c, key_lanes)]

    def turn_part(part):
        load_part(part).wait()
        for j in range(load_rows):
            r = part * load_rows + j
            for h in range(HALVES):
                for k in range(per_block):
                    block = tiles[r, k, :, h * half:(h + 1) * half]
                    turned[r, h, k * half:(k + 1) * half, :] = jnp.transpose(block)

    def adjoint(turn):
        with scope(f"g{turn}"):
            for start in range(0, cols, GROUP):
                group = col_peers[start:start + GROUP]
                for p in group:
                    if p is not col_peers[0]:
                        left_copy(turn, p, p).wait_recv()
                products = []
                for p in group:
                    for i in range(rays):
                        r = p * rays + i
                        row = left_panel[turn, p, i]
                        for k in range(per_block):
                            term = jnp.dot(row, tiles[r, k], preferred_element_type=f32)
                            products.append((1 + k * row_tiles + r, term))
                for t, term in products:
                    for h in range(HALVES):
                        terms[h, t] = term[:, h * half:(h + 1) * half]
        with scope(f"chain{turn}"):
            squares = jnp.zeros((sides, half), f32)
            for p in range(cols):
                squares = squares + left_panel[turn, p, rays, :, :half].astype(f32)
                squares = squares + left_panel[turn, p, rays, :, half:].astype(f32)
            high, low = split(squares)
            for h in range(HALVES):
                terms[h, 0] = jnp.zeros((sides, half), f32)

            def chain(r, k):
                before = table_ref[key_rows + k, r]
                for h in range(HALVES):
                    terms[h, 1 + k * row_tiles + r] = terms[h, 1 + k * row_tiles + r] + terms[h, before]

            for k in range(per_block):
                tile_loop(row_tiles, row_tiles, lambda r: chain(r, k))
        with scope(f"sendsums{turn}"):
            for h in range(HALVES):
                for p in reversed(row_peers[1:]):
                    for i in range(own):
                        voxel_send[turn, h, p, i] = terms[h, last_term(p * own + i)].astype(bf16)
                    if h == 0:
                        voxel_send[turn, h, p, own] = high
                        voxel_send[turn, h, p, own + 1] = low
                    sums_copy(turn, h, p, p, me_row).start()
        voxel_recv[turn, 0, me_row, own] = high
        voxel_recv[turn, 0, me_row, own + 1] = low

    def sums_copy(turn, h, peer, source, slot):
        size = pl.ds(0, own + 2 if h == 0 else own)
        return copy_to(
            "row", peer, voxel_send.at[turn, h, source, size], voxel_recv.at[turn, h, slot, size],
            vs_send_sem.at[turn, h, peer], vs_recv_sem.at[turn, h, slot],
        )

    def voxel_copy(turn, h, peer, slot):
        return copy_to(
            "row", peer, voxel_panel[turn][h].at[slot], voxel_panel[turn][h].at[slot],
            vp_send_sem.at[turn, h, peer], vp_recv_sem.at[turn, h, slot],
        )

    def low_copy(peer, source, slot):
        return copy_to(
            "row", peer, low_send.at[source], low_recv.at[slot], lo_send_sem.at[peer], lo_recv_sem.at[slot]
        )

    def fill_low():
        for p in row_peers[1:]:
            for h in range(HALVES):
                for i in range(own):
                    term = terms[h, last_term(p * own + i)]
                    low_send[p, h, i] = (term - voxel_send[0, h, p, i].astype(f32)).astype(bf16)

    near_rows = row_peers[1:rows // 2]
    far_rows = row_peers[rows // 2:]

    def send_low(peers):
        for p in peers:
            low_copy(p, p, me_row).start()

    def add_low(inverse):
        for p in row_peers[1:]:
            low_copy(p, p, p).wait_recv()

        def one(i):
            for h in range(HALVES):
                total = low_recv[row_peers[1], h, i].astype(f32)
                for p in row_peers[2:]:
                    total = total + low_recv[p, h, i].astype(f32)
                lanes = pl.ds(pl.multiple_of(i * tile_size + h * half, half), half)
                first_ref[:, lanes] = first_ref[:, lanes] + total * inverse

        tile_loop(own, 4, one)

    right_refs = (first_ref, second_ref)

    def finish_right(turn, beta_of, alpha_before):
        beta = None
        for h in range(HALVES):
            with scope(f"waitsums{turn}{h}"):
                for p in row_peers[1:]:
                    sums_copy(turn, h, p, p, p).wait_recv()
            if h == 0:
                beta, inverse, pull = beta_of()
            with scope(f"right{turn}{h}"):
                def one(i, squares, h=h):
                    total = terms[h, last_term(me_row * own + i)]
                    for p in row_peers[1:]:
                        total = total + voxel_recv[turn, h, p, i].astype(f32)
                    lanes = pl.ds(pl.multiple_of(i * tile_size + h * half, half), half)
                    right_raw = total * inverse
                    if turn > 0:
                        right_raw = right_raw - pull * right_refs[turn - 1][:, lanes]
                    right_refs[turn][:, lanes] = right_raw
                    voxel_panel[turn][h][me_row, i] = right_raw.astype(bf16)
                    return squares + right_raw * right_raw

                def step(base, squares):
                    for j in range(4):
                        squares = one(base * 4 + j, squares)
                    return squares

                squares = lax.fori_loop(0, own // 4, step, jnp.zeros((sides, half), f32))
                high, low = split(squares)
                voxel_panel[turn][h][me_row, own] = high
                voxel_panel[turn][h][me_row, own + 1] = low
                for p in reversed(row_peers[1:]):
                    voxel_copy(turn, h, p, me_row).start()
        return beta

    def beta_over_row(turn):
        total = jnp.zeros((sides, half), f32)
        for p in range(rows):
            total = total + voxel_recv[turn, 0, p, own].astype(f32)
            total = total + voxel_recv[turn, 0, p, own + 1].astype(f32)
        return norm_of(total)

    def ray_copy(turn, peer, source, slot):
        return copy_to(
            "col", peer, ray_send.at[turn, source], ray_recv.at[turn, slot],
            rs_send_sem.at[turn, peer], rs_recv_sem.at[turn, slot],
        )

    def picked(turn, h, r):
        pieces = []
        for k in range(per_block):
            c = cols_ref[k, r]
            pieces.append(voxel_panel[turn][h][lax.div(c, own), lax.rem(c, own)])
        return jnp.concatenate(pieces, axis=1)

    def forward(turn):
        with scope(f"waitvox{turn}0"):
            for p in row_peers[1:]:
                voxel_copy(turn, 0, p, p).wait_recv()
        with scope(f"f{turn}0"):
            def early(r):
                ray_part[r] = jnp.dot(picked(turn, 0, r), turned[r, 0], preferred_element_type=f32)

            tile_loop(row_tiles, min(8, row_tiles), early)
        with scope(f"waitvox{turn}1"):
            for p in row_peers[1:]:
                voxel_copy(turn, 1, p, p).wait_recv()
        with scope(f"f{turn}1"):
            squares = jnp.zeros((sides, half), f32)
            for h in range(HALVES):
                for p in range(rows):
                    squares = squares + voxel_panel[turn][h][p, own].astype(f32)
                    squares = squares + voxel_panel[turn][h][p, own + 1].astype(f32)
            farthest = col_peers[::-1]
            for start in range(0, cols, GROUP):
                group = farthest[start:start + GROUP]
                products = []
                for p in group:
                    for i in range(rays):
                        r = p * rays + i
                        total = ray_part[r] + jnp.dot(picked(turn, 1, r), turned[r, 1], preferred_element_type=f32)
                        products.append((p, i, total))
                for p, i, total in products:
                    for h in range(HALVES):
                        ray_send[turn, p, HALVES * i + h] = total[:, h * half:(h + 1) * half]
                for p in group:
                    if p is not col_peers[0]:
                        ray_send[turn, p, HALVES * rays] = squares
                        ray_copy(turn, p, p, me_col).start()
            if turn == 0:
                send_low(near_rows)
            ray_recv[turn, me_col, HALVES * rays] = squares
        with scope(f"waitrays{turn}"):
            pieces = [ray_send[turn, me_col, i] for i in range(HALVES * rays)]
            for p in col_peers[1:]:
                ray_copy(turn, p, p, p).wait_recv()
                for i in range(HALVES * rays):
                    pieces[i] = pieces[i] + ray_recv[turn, p, i]
            squares = ray_recv[turn, 0, HALVES * rays]
            for p in range(1, cols):
                squares = squares + ray_recv[turn, p, HALVES * rays]
        sums = [jnp.concatenate(pieces[HALVES * i:HALVES * (i + 1)], axis=1) for i in range(rays)]
        return sums, norm_of(squares)

    def wide(value):
        return jnp.concatenate([value] * HALVES, axis=1)

    loads[0].wait()
    publish_left(0, [side_tile(i) for i in range(rays)])
    with scope("barrier"):
        pl.semaphore_wait(barrier, rows - 1 + cols - 1)
    send_left(0)
    with scope("table"):
        loads[1].wait()
        loads[2].wait()
        make_table()
    with scope("turn"):
        for part in range(LOAD_PARTS):
            turn_part(part)
    adjoint(0)
    with scope("fill"):
        fill_low()

    def first_beta():
        beta = beta_over_row(0)
        return beta, 1.0 / beta, None

    beta0 = finish_right(0, first_beta, None)
    sums, alpha0 = forward(0)
    alpha = wide(alpha0)
    beta = wide(beta0)
    left_raw = [sums[i] / alpha - alpha * (side_tile(i) / beta) for i in range(rays)]
    for i in range(rays):
        left_ref[i] = left_raw[i]
    publish_left(1, left_raw)
    send_left(1)
    send_low(far_rows)
    adjoint(1)
    with scope("addlow"):
        add_low(1.0 / beta0)

    def second_beta():
        beta = beta_over_row(1)
        return beta, 1.0 / beta, beta / alpha0

    beta1 = finish_right(1, second_beta, alpha0)
    rho1 = jnp.sqrt(alpha0 * alpha0 + beta1 * beta1)
    cosine1 = alpha0 / rho1
    sine1 = beta1 / rho1
    phi1 = cosine1 * beta0
    phibar1 = sine1 * beta0
    sums, alpha1 = forward(1)
    theta1 = sine1 * alpha1
    rhobar1 = -cosine1 * alpha1
    alpha = wide(alpha1)
    beta = wide(beta1)
    left_raw = [sums[i] / alpha - alpha * (left_ref[i] / beta) for i in range(rays)]
    for i in range(rays):
        left_ref[i] = left_raw[i]

    parts = 2 if cols == 16 else 1
    inner = cols // parts
    my_part = lax.div(me_col, inner)
    my_place = lax.rem(me_col, inner)
    place_peers = [(me_row, p, lax.rem(p, inner)) for p in col_peers[1:inner]]
    part_peers = []
    for d in range(parts):
        part = lax.rem(my_part + d, parts)
        for p in row_peers if d else row_peers[1:]:
            part_peers.append((p, part * inner + my_place, part * rows + p))

    def norm_copy(ref, peer, slot, send_sem, recv_sem):
        return pltpu.make_async_remote_copy(
            src_ref=ref.at[slot], dst_ref=ref.at[slot], send_sem=send_sem.at[peer[2]], recv_sem=recv_sem.at[slot],
            device_id={"row": peer[0], "col": peer[1]}, device_id_type=MESH,
        )

    def all_sum(ref, peers, me, value, send_sem, recv_sem):
        ref[me] = value
        for peer in reversed(peers):
            norm_copy(ref, peer, me, send_sem, recv_sem).start()
        for peer in peers:
            norm_copy(ref, peer, peer[2], send_sem, recv_sem).wait_recv()
        total = ref[0]
        for p in range(1, len(peers) + 1):
            total = total + ref[p]
        return total

    squares = fold(sum_of_squares(left_raw))
    with scope("normcol"):
        squares = all_sum(norm_col, place_peers, my_place, squares, nc_send_sem, nc_recv_sem)
    with scope("normrow"):
        squares = all_sum(norm_row, part_peers, my_part * rows + me_row, squares, nr_send_sem, nr_recv_sem)
    beta2 = norm_of(squares)
    rho2 = jnp.sqrt(rhobar1 * rhobar1 + beta2 * beta2)
    cosine2 = rhobar1 / rho2
    sine2 = beta2 / rho2
    phi2 = cosine2 * phibar1
    phibar2 = sine2 * phibar1
    for i, value in enumerate((
        alpha0, alpha1, phi1 / rho1, theta1 / rho1, phi2 / rho2, phibar2 / beta0, beta2, rho2, cosine2, sine2
    )):
        stats_ref[i] = value
    with scope("drain"):
        def drain_row(p):
            for turn in range(ITERS):
                for h in range(HALVES):
                    sums_copy(turn, h, p, p, me_row).wait_send()
                    voxel_copy(turn, h, p, me_row).wait_send()
            low_copy(p, p, me_row).wait_send()

        def drain_col(p):
            for turn in range(ITERS):
                left_copy(turn, p, me_col).wait_send()
                ray_copy(turn, p, p, me_col).wait_send()

        each(me_row, rows, drain_row)
        each(me_col, cols, drain_col)
        for peer in place_peers:
            norm_copy(norm_col, peer, my_place, nc_send_sem, nc_recv_sem).wait_send()
        for peer in part_peers:
            norm_copy(norm_row, peer, my_part * rows + me_row, nr_send_sem, nr_recv_sem).wait_send()


def local(observed, tile_values, tile_cols):
    sides = observed.shape[0]
    row_tiles = tile_values.shape[0]
    per_block = tile_values.shape[1]
    tile_size = tile_values.shape[2]
    rows = lax.axis_size("row")
    cols = lax.axis_size("col")
    col_tiles = N // (tile_size * cols)
    panel_len = col_tiles * tile_size
    own = col_tiles // rows
    rays = row_tiles // cols
    flat = row_tiles * per_block
    half = tile_size // HALVES
    key_lanes = min(col_tiles, 128)
    key_rows = col_tiles // key_lanes

    f32 = jnp.float32
    bf16 = tile_values.dtype
    share_len = own * tile_size
    dma = pltpu.SemaphoreType.DMA
    voxel_shape = (ITERS, HALVES, rows, own + 2, sides, half)
    ray_shape = (ITERS, cols, HALVES * rays + 1, sides, half)
    scratch = [
        pltpu.VMEM(observed.shape, f32),
        pltpu.SMEM(tile_cols.shape[::-1], jnp.int32),
        pltpu.VMEM(tile_cols.shape[::-1], jnp.int32),
        pltpu.VMEM(tile_values.shape, bf16),
        pltpu.VMEM((row_tiles, HALVES, per_block * half, tile_size), bf16),
        pltpu.VMEM((HALVES, 1 + flat, sides, half), f32),
        pltpu.VMEM((row_tiles, sides, tile_size), f32),
        pltpu.VMEM((ITERS, cols, rays + 1, sides, tile_size), bf16),
        [[pltpu.VMEM(voxel_shape[2:], bf16) for _ in range(HALVES)] for _ in range(ITERS)],
        pltpu.VMEM(voxel_shape, bf16),
        pltpu.VMEM(voxel_shape, bf16),
        pltpu.VMEM((rows, HALVES, own, sides, half), bf16),
        pltpu.VMEM((rows, HALVES, own, sides, half), bf16),
        pltpu.VMEM(ray_shape, COL_SUM),
        pltpu.VMEM(ray_shape, COL_SUM),
        pltpu.VMEM((cols, sides, half), f32),
        pltpu.VMEM((2 * rows, sides, half), f32),
        pltpu.VMEM((key_rows + per_block, key_lanes), jnp.int32),
        pltpu.SMEM((key_rows + per_block, key_lanes), jnp.int32),
        dma((3,)), dma((LOAD_PARTS,)), dma,
        dma((ITERS, cols)), dma((ITERS, cols)),
        dma((ITERS, HALVES, rows)), dma((ITERS, HALVES, rows)),
        dma((ITERS, HALVES, rows)), dma((ITERS, HALVES, rows)),
        dma((rows,)), dma((rows,)),
        dma((ITERS, cols)), dma((ITERS, cols)),
        dma((cols,)), dma((cols,)),
        dma((2 * rows,)), dma((2 * rows,)),
    ]
    vmem = pl.BlockSpec(memory_space=pltpu.VMEM)
    hbm = pl.BlockSpec(memory_space=pltpu.HBM)
    columns = jnp.transpose(tile_cols)
    first_raw, second_raw, left_raw, stats = pl.pallas_call(
        functools.partial(solver_kernel, rows, cols, rays, own),
        out_shape=(
            jax.ShapeDtypeStruct((sides, share_len), f32),
            jax.ShapeDtypeStruct((sides, share_len), f32),
            jax.ShapeDtypeStruct((rays, sides, tile_size), f32),
            jax.ShapeDtypeStruct((10, sides, half), f32),
        ),
        in_specs=[hbm, hbm, hbm],
        out_specs=(vmem, vmem, vmem, vmem),
        scratch_shapes=scratch,
        compiler_params=pltpu.CompilerParams(
            collective_id=0, has_side_effects=True, vmem_limit_bytes=57 * 1024 * 1024
        ),
    )(observed, columns, tile_values)

    alpha0, alpha1, step1, turn1, step2, residual_ratio, beta2, rho2, cosine2, sine2 = (
        stats[i, :, :1] for i in range(10)
    )
    direction = first_raw / alpha0
    solution = step1 * direction
    right_vec = second_raw / alpha1
    direction = right_vec - turn1 * direction
    solution = solution + step2 * direction

    left_bf = jnp.transpose(left_raw, (1, 0, 2)).reshape(sides, -1).astype(bf16)
    gathered = lax.all_gather(left_bf, "col", axis=1, tiled=True).reshape(sides, row_tiles, tile_size)
    tile_terms = jnp.einsum("rktj,nrt->nrkj", tile_values, gathered, preferred_element_type=f32)
    placed = (
        jnp.zeros((sides, col_tiles, tile_size), f32)
        .at[:, tile_cols.reshape(-1)]
        .add(tile_terms.reshape(sides, flat, tile_size))
        .reshape(sides, panel_len)
    )
    product = lax.psum_scatter(placed, "row", scatter_dimension=1, tiled=True)
    last_raw = product / beta2 - beta2 * right_vec
    alpha2 = jnp.sqrt(lax.psum(jnp.sum(last_raw * last_raw, axis=1), ("row", "col")) + epsilon_sq)[:, None]
    theta2 = sine2 * alpha2
    rhobar2 = -cosine2 * alpha2
    direction = last_raw / alpha2 - (theta2 / rho2) * direction
    del direction, rhobar2
    return (solution, residual_ratio[:, 0])


def solution(mesh):
    in_specs = (P(None, ("row", "col")), P("row", "col", None, None), P("row", "col"))
    out_specs = (P(None, ("col", "row")), P())
    return jax.shard_map(local, mesh=mesh, in_specs=in_specs, out_specs=out_specs, check_vma=False)
```

time: 1160 us -> 78.8 us (0.07)
  blocking collectives: 1050 us -> 0 us
  Pallas kernels: 0 us -> 74.9 us
  local copies, waits for them, and re-layouts: 48 us -> 1.32 us
  matrix products: 20.5 us -> 0 us
  waiting for transfers between devices: 16.2 us -> 0 us
  between operations: 13.9 us -> 0.64 us
    psum x5 -> x0, blocking collectives: 957 us -> none  [the longest x3 807 us: lanczos_pair(): beta_sq = lax.psum(jnp.sum(left_raw * left_raw, axis=1), ('row', 'col'))]
    all_gather x4 -> x0, blocking collectives: 95.5 us -> none  [the longest x2 49.7 us: adjoint_map(): lax.all_gather(left_bf, 'col', axis=1, tiled=True)]
    pallas_call x0 -> x1, Pallas kernels: none -> 74.9 us  [local(): pl.pallas_call(functools.partial(solver_kernel, rows, cols, rays, own), o...]
    unnamed x13 -> x0, local copies, waits for them, and re-layouts: 46 us -> none
    dot_general x4 -> x0, matrix products: 20.5 us -> none  [the longest x2 11.3 us: local(): jnp.einsum('rktj,nrkj->nrt', tile_values, picked, preferred_element_type=...]
    unnamed x8 -> x0, waiting for transfers between devices: 16.2 us -> none
  transfers between devices with their start and end apart: 4 -> 0, of which waited for: 2 -> 0; matrix products, arithmetic and copies ran while one was open for 0% -> 0% of each run, Pallas kernels for 0% -> 0%
where the time goes in v1:
time: 78.8 us; the launch traced here: 78.6 us
  Pallas kernels  74.9 us (95%)
  other arithmetic  1.76 us (2%)
  local copies, waits for them, and re-layouts  1.32 us (2%)
    pallas_call x1, Pallas kernels, local(): pl.pallas_call(functools.partial(solver_kernel, rows, cols, rays, own), o...  74.9 us
    add x1, other arithmetic, local(): solution = solution + step2 * direction  1.76 us

profile of v1, /device:TPU:1, one launch (start us, length us, event | category | flops | bytes accessed | tf_op | source)
XLA Modules:
  0.0 78.6 jit_solution(2383595181835743496)
XLA Ops:
  0.6 74.9 %shard_map.50 = (f32[4,8192]{1,0:T(4,128)}, f32[4,8192]{1,0:T(4,128)}, f32[2,4,256]{2,1,0:T(4,128)}, f32[10,4,128]{2,1,0:T(4,128)}) custom-call(f32[4,512]{1,0:T(4,128)} %observed_hbm.1, s32[2,32]{1,0:T(2,128)} %bitcast.1, bf16[32,2,256,256]{3,2,1,0:T(8,128)(2,1)} %tiles_hbm.1), custom_call_target="tpu_custom_call" | custom-call | tf_op jit(solution)/shard_map/pallas_call | solution.py:555
  75.5 1.3 %slice_reduce_fusion = (f32[4]{0:T(128)}, f32[4]{0:T(128)S(1)}, f32[4]{0:T(128)S(1)}, f32[4]{0:T(128)S(1)}, f32[4]{0:T(128)S(1)}, /*index=5*/f32[4]{0:T(128)S(1)}) fusion(f32[10,4,128]{2,1,0:T(4,128)} %get-tuple-element.5), kind=kLoop, calls=%fused_computation.2 | loop fusion | bytes 192 | tf_op jit(solution)/shard_map/slice | solution.py:572
  76.8 1.8 %multiply_add_fusion = f32[4,8192]{1,0:T(4,128)} fusion(f32[4,8192]{1,0:T(4,128)} %get-tuple-element.7, f32[4,8192]{1,0:T(4,128)} %get-tuple-element.6, f32[4]{0:T(128)S(1)} %get-tuple-element.9, f32[4]{0:T(128)S(1)} %get-tuple-element.10, f32[4]{0:T(128)S(1)} %get-tuple-element.11, f32[4]{0:T(128)S(1)} %get-tuple-element.12, f32[4]{0:T(128)S(1)} %get-tuple-element.13), kind=kLoop, calls=%fused_computation.1 | loop fusion | flops 229376 | bytes 393296 | tf_op jit(solution)/shard_map/add | solution.py:578

commit v2 on v1

--- a/solution.py
+++ b/solution.py
@@ -60,11 +60,11 @@
 
 def solver_kernel(
     rows, cols, rays, own,
-    observed_hbm, columns_hbm, tiles_hbm,
+    observed_ref, cols_vec, tiles_hbm,
     first_ref, second_ref, left_ref, stats_ref,
-    observed_ref, cols_ref, cols_vec, tiles, turned, terms, ray_part, left_panel, voxel_panel, voxel_send, voxel_recv, low_send, low_recv,
+    cols_ref, tiles, turned, terms, ray_part, left_panel, voxel_panel, voxel_send, voxel_recv, low_send, low_recv,
     ray_send, ray_recv, norm_col, norm_row, table_vec, table_ref,
-    input_sem, load_sem, table_sem, lp_send_sem, lp_recv_sem, vs_send_sem, vs_recv_sem, vp_send_sem, vp_recv_sem,
+    columns_sem, load_sem, table_sem, lp_send_sem, lp_recv_sem, vs_send_sem, vs_recv_sem, vp_send_sem, vp_recv_sem,
     lo_send_sem, lo_recv_sem, rs_send_sem, rs_recv_sem, nc_send_sem, nc_recv_sem, nr_send_sem, nr_recv_sem,
 ):
     f32 = jnp.float32
@@ -119,13 +119,8 @@
         piece = pl.ds(part * load_rows, load_rows)
         return pltpu.make_async_copy(tiles_hbm.at[piece], tiles.at[piece], load_sem.at[part])
 
-    loads = (
-        pltpu.make_async_copy(observed_hbm, observed_ref, input_sem.at[0]),
-        pltpu.make_async_copy(columns_hbm, cols_ref, input_sem.at[1]),
-        pltpu.make_async_copy(columns_hbm, cols_vec, input_sem.at[2]),
-    )
-    for load in loads:
-        load.start()
+    columns_load = pltpu.make_async_copy(cols_vec, cols_ref, columns_sem)
+    columns_load.start()
     for part in range(LOAD_PARTS):
         load_part(part).start()
 
@@ -142,7 +137,7 @@
     def left_copy(turn, peer, slot):
         return copy_to(
             "col", peer, left_panel.at[turn, slot], left_panel.at[turn, slot],
-            lp_send_sem.at[turn, peer], lp_recv_sem.at[turn, slot],
+            lp_send_sem, lp_recv_sem.at[slot],
         )
 
     def send_left(turn):
@@ -231,18 +226,45 @@
         size = pl.ds(0, own + 2 if h == 0 else own)
         return copy_to(
             "row", peer, voxel_send.at[turn, h, source, size], voxel_recv.at[turn, h, slot, size],
-            vs_send_sem.at[turn, h, peer], vs_recv_sem.at[turn, h, slot],
+            vs_send_sem.at[h], vs_recv_sem.at[h],
         )
 
     def voxel_copy(turn, h, peer, slot):
         return copy_to(
             "row", peer, voxel_panel[turn][h].at[slot], voxel_panel[turn][h].at[slot],
-            vp_send_sem.at[turn, h, peer], vp_recv_sem.at[turn, h, slot],
-        )
-
-    def low_copy(peer, source, slot):
-        return copy_to(
-            "row", peer, low_send.at[source], low_recv.at[slot], lo_send_sem.at[peer], lo_recv_sem.at[slot]
+            vp_send_sem.at[h], vp_recv_sem.at[h],
+        )
+
+    def all_left(turn):
+        whole = left_panel.at[turn, pl.ds(0, cols - 1)]
+        return copy_to("col", col_peers[1], whole, whole, lp_send_sem, lp_recv_sem.at[0])
+
+    def all_sums(turn, h):
+        size = pl.ds(0, own + 2 if h == 0 else own)
+        return copy_to(
+            "row", row_peers[1], voxel_send.at[turn, h, pl.ds(0, rows - 1), size],
+            voxel_recv.at[turn, h, pl.ds(0, rows - 1), size], vs_send_sem.at[h], vs_recv_sem.at[h],
+        )
+
+    def all_voxels(turn, h):
+        whole = voxel_panel[turn][h].at[pl.ds(0, rows - 1)]
+        return copy_to("row", row_peers[1], whole, whole, vp_send_sem.at[h], vp_recv_sem.at[h])
+
+    def all_rays(turn):
+        return copy_to(
+            "col", col_peers[1], ray_send.at[turn, pl.ds(0, cols - 1)], ray_recv.at[turn, pl.ds(0, cols - 1)],
+            rs_send_sem, rs_recv_sem,
+        )
+
+    def all_low(group):
+        size = pl.ds(0, len(low_groups[group]))
+        return copy_to(
+            "row", row_peers[1], low_send.at[size], low_recv.at[size], lo_send_sem.at[group], lo_recv_sem.at[group]
+        )
+
+    def low_copy(group, peer, source, slot):
+        return copy_to(
+            "row", peer, low_send.at[source], low_recv.at[slot], lo_send_sem.at[group], lo_recv_sem.at[group]
         )
 
     def fill_low():
@@ -252,24 +274,30 @@
                     term = terms[h, last_term(p * own + i)]
                     low_send[p, h, i] = (term - voxel_send[0, h, p, i].astype(f32)).astype(bf16)
 
-    near_rows = row_peers[1:rows // 2]
-    far_rows = row_peers[rows // 2:]
-
-    def send_low(peers):
-        for p in peers:
-            low_copy(p, p, me_row).start()
-
-    def add_low(inverse):
-        for p in row_peers[1:]:
-            low_copy(p, p, p).wait_recv()
+    low_groups = (row_peers[1:max(rows // 2, 1)], row_peers[max(rows // 2, 1):])
+
+    def send_low(group):
+        for p in low_groups[group]:
+            low_copy(group, p, p, me_row).start()
+
+    def low_sum(group, h, i):
+        total = low_recv[low_groups[group][0], h, i].astype(f32)
+        for p in low_groups[group][1:]:
+            total = total + low_recv[p, h, i].astype(f32)
+        return total
+
+    def add_low(group, inverse, pull=None):
+        if not low_groups[group]:
+            return
+        all_low(group).wait_recv()
 
         def one(i):
             for h in range(HALVES):
-                total = low_recv[row_peers[1], h, i].astype(f32)
-                for p in row_peers[2:]:
-                    total = total + low_recv[p, h, i].astype(f32)
                 lanes = pl.ds(pl.multiple_of(i * tile_size + h * half, half), half)
-                first_ref[:, lanes] = first_ref[:, lanes] + total * inverse
+                change = low_sum(group, h, i) * inverse
+                first_ref[:, lanes] = first_ref[:, lanes] + change
+                if pull is not None:
+                    second_ref[:, lanes] = second_ref[:, lanes] - pull * change
 
         tile_loop(own, 4, one)
 
@@ -279,8 +307,7 @@
         beta = None
         for h in range(HALVES):
             with scope(f"waitsums{turn}{h}"):
-                for p in row_peers[1:]:
-                    sums_copy(turn, h, p, p, p).wait_recv()
+                all_sums(turn, h).wait_recv()
             if h == 0:
                 beta, inverse, pull = beta_of()
             with scope(f"right{turn}{h}"):
@@ -319,7 +346,7 @@
     def ray_copy(turn, peer, source, slot):
         return copy_to(
             "col", peer, ray_send.at[turn, source], ray_recv.at[turn, slot],
-            rs_send_sem.at[turn, peer], rs_recv_sem.at[turn, slot],
+            rs_send_sem, rs_recv_sem,
         )
 
     def picked(turn, h, r):
@@ -331,16 +358,14 @@
 
     def forward(turn):
         with scope(f"waitvox{turn}0"):
-            for p in row_peers[1:]:
-                voxel_copy(turn, 0, p, p).wait_recv()
+            all_voxels(turn, 0).wait_recv()
         with scope(f"f{turn}0"):
             def early(r):
                 ray_part[r] = jnp.dot(picked(turn, 0, r), turned[r, 0], preferred_element_type=f32)
 
             tile_loop(row_tiles, min(8, row_tiles), early)
         with scope(f"waitvox{turn}1"):
-            for p in row_peers[1:]:
-                voxel_copy(turn, 1, p, p).wait_recv()
+            all_voxels(turn, 1).wait_recv()
         with scope(f"f{turn}1"):
             squares = jnp.zeros((sides, half), f32)
             for h in range(HALVES):
@@ -364,12 +389,12 @@
                         ray_send[turn, p, HALVES * rays] = squares
                         ray_copy(turn, p, p, me_col).start()
             if turn == 0:
-                send_low(near_rows)
+                send_low(0)
             ray_recv[turn, me_col, HALVES * rays] = squares
         with scope(f"waitrays{turn}"):
             pieces = [ray_send[turn, me_col, i] for i in range(HALVES * rays)]
+            all_rays(turn).wait_recv()
             for p in col_peers[1:]:
-                ray_copy(turn, p, p, p).wait_recv()
                 for i in range(HALVES * rays):
                     pieces[i] = pieces[i] + ray_recv[turn, p, i]
             squares = ray_recv[turn, 0, HALVES * rays]
@@ -381,14 +406,19 @@
     def wide(value):
         return jnp.concatenate([value] * HALVES, axis=1)
 
-    loads[0].wait()
+    def drain(turn):
+        all_left(turn).wait_send()
+        for h in range(HALVES):
+            all_sums(turn, h).wait_send()
+            all_voxels(turn, h).wait_send()
+        all_rays(turn).wait_send()
+
     publish_left(0, [side_tile(i) for i in range(rays)])
     with scope("barrier"):
         pl.semaphore_wait(barrier, rows - 1 + cols - 1)
     send_left(0)
     with scope("table"):
-        loads[1].wait()
-        loads[2].wait()
+        columns_load.wait()
         make_table()
     with scope("turn"):
         for part in range(LOAD_PARTS):
@@ -409,11 +439,11 @@
     for i in range(rays):
         left_ref[i] = left_raw[i]
     publish_left(1, left_raw)
+    drain(0)
     send_left(1)
-    send_low(far_rows)
     adjoint(1)
     with scope("addlow"):
-        add_low(1.0 / beta0)
+        add_low(0, 1.0 / beta0)
 
     def second_beta():
         beta = beta_over_row(1)
@@ -447,7 +477,7 @@
 
     def norm_copy(ref, peer, slot, send_sem, recv_sem):
         return pltpu.make_async_remote_copy(
-            src_ref=ref.at[slot], dst_ref=ref.at[slot], send_sem=send_sem.at[peer[2]], recv_sem=recv_sem.at[slot],
+            src_ref=ref.at[slot], dst_ref=ref.at[slot], send_sem=send_sem, recv_sem=recv_sem,
             device_id={"row": peer[0], "col": peer[1]}, device_id_type=MESH,
         )
 
@@ -455,18 +485,20 @@
         ref[me] = value
         for peer in reversed(peers):
             norm_copy(ref, peer, me, send_sem, recv_sem).start()
-        for peer in peers:
-            norm_copy(ref, peer, peer[2], send_sem, recv_sem).wait_recv()
+        norm_copy(ref, peers[0], pl.ds(0, len(peers)), send_sem, recv_sem).wait()
         total = ref[0]
         for p in range(1, len(peers) + 1):
             total = total + ref[p]
         return total
 
     squares = fold(sum_of_squares(left_raw))
+    send_low(1)
     with scope("normcol"):
         squares = all_sum(norm_col, place_peers, my_place, squares, nc_send_sem, nc_recv_sem)
     with scope("normrow"):
         squares = all_sum(norm_row, part_peers, my_part * rows + me_row, squares, nr_send_sem, nr_recv_sem)
+    with scope("addlow2"):
+        add_low(1, 1.0 / beta0, beta1 / alpha0)
     beta2 = norm_of(squares)
     rho2 = jnp.sqrt(rhobar1 * rhobar1 + beta2 * beta2)
     cosine2 = rhobar1 / rho2
@@ -478,24 +510,10 @@
     )):
         stats_ref[i] = value
     with scope("drain"):
-        def drain_row(p):
-            for turn in range(ITERS):
-                for h in range(HALVES):
-                    sums_copy(turn, h, p, p, me_row).wait_send()
-                    voxel_copy(turn, h, p, me_row).wait_send()
-            low_copy(p, p, me_row).wait_send()
-
-        def drain_col(p):
-            for turn in range(ITERS):
-                left_copy(turn, p, me_col).wait_send()
-                ray_copy(turn, p, p, me_col).wait_send()
-
-        each(me_row, rows, drain_row)
-        each(me_col, cols, drain_col)
-        for peer in place_peers:
-            norm_copy(norm_col, peer, my_place, nc_send_sem, nc_recv_sem).wait_send()
-        for peer in part_peers:
-            norm_copy(norm_row, peer, my_part * rows + me_row, nr_send_sem, nr_recv_sem).wait_send()
+        drain(1)
+        for group in range(2):
+            if low_groups[group]:
+                all_low(group).wait_send()
 
 
 def local(observed, tile_values, tile_cols):
@@ -521,9 +539,7 @@
     voxel_shape = (ITERS, HALVES, rows, own + 2, sides, half)
     ray_shape = (ITERS, cols, HALVES * rays + 1, sides, half)
     scratch = [
-        pltpu.VMEM(observed.shape, f32),
         pltpu.SMEM(tile_cols.shape[::-1], jnp.int32),
-        pltpu.VMEM(tile_cols.shape[::-1], jnp.int32),
         pltpu.VMEM(tile_values.shape, bf16),
         pltpu.VMEM((row_tiles, HALVES, per_block * half, tile_size), bf16),
         pltpu.VMEM((HALVES, 1 + flat, sides, half), f32),
@@ -540,17 +556,16 @@
         pltpu.VMEM((2 * rows, sides, half), f32),
         pltpu.VMEM((key_rows + per_block, key_lanes), jnp.int32),
         pltpu.SMEM((key_rows + per_block, key_lanes), jnp.int32),
-        dma((3,)), dma((LOAD_PARTS,)), dma,
-        dma((ITERS, cols)), dma((ITERS, cols)),
-        dma((ITERS, HALVES, rows)), dma((ITERS, HALVES, rows)),
-        dma((ITERS, HALVES, rows)), dma((ITERS, HALVES, rows)),
-        dma((rows,)), dma((rows,)),
-        dma((ITERS, cols)), dma((ITERS, cols)),
-        dma((cols,)), dma((cols,)),
-        dma((2 * rows,)), dma((2 * rows,)),
+        dma, dma((LOAD_PARTS,)), dma,
+        dma, dma((cols,)),
+        dma((HALVES,)), dma((HALVES,)),
+        dma((HALVES,)), dma((HALVES,)),
+        dma((2,)), dma((2,)),
+        dma, dma,
+        dma, dma,
+        dma, dma,
     ]
     vmem = pl.BlockSpec(memory_space=pltpu.VMEM)
-    hbm = pl.BlockSpec(memory_space=pltpu.HBM)
     columns = jnp.transpose(tile_cols)
     first_raw, second_raw, left_raw, stats = pl.pallas_call(
         functools.partial(solver_kernel, rows, cols, rays, own),
@@ -560,11 +575,11 @@
             jax.ShapeDtypeStruct((rays, sides, tile_size), f32),
             jax.ShapeDtypeStruct((10, sides, half), f32),
         ),
-        in_specs=[hbm, hbm, hbm],
+        in_specs=[vmem, vmem, pl.BlockSpec(memory_space=pltpu.HBM)],
         out_specs=(vmem, vmem, vmem, vmem),
         scratch_shapes=scratch,
         compiler_params=pltpu.CompilerParams(
-            collective_id=0, has_side_effects=True, vmem_limit_bytes=57 * 1024 * 1024
+            collective_id=0, has_side_effects=True, vmem_limit_bytes=53 * 1024 * 1024
         ),
     )(observed, columns, tile_values)
 

time: 78.8 us -> 73.5 us (0.933)
  Pallas kernels: 74.9 us -> 69.9 us
  other arithmetic: 1.76 us -> 0.79 us
    pallas_call x1, Pallas kernels: 74.9 us -> 69.9 us  [local(): pl.pallas_call(functools.partial(solver_kernel, rows, cols, rays, own), o...]
    unnamed x0 -> x4, local copies, waits for them, and re-layouts: none -> 1.37 us
    add x1, other arithmetic: 1.76 us -> 0.79 us  [local(): solution = solution + step2 * direction]
where the time goes in v2:
time: 73.5 us; the launch traced here: 73.4 us
  Pallas kernels  69.9 us (95%)
  local copies, waits for them, and re-layouts  2 us (3%)
  other arithmetic  0.79 us (1%)
    pallas_call x1, Pallas kernels, local(): pl.pallas_call(functools.partial(solver_kernel, rows, cols, rays, own), o...  69.9 us

profile of v2, /device:TPU:1, one launch (start us, length us, event | category | flops | bytes accessed | tf_op | source)
XLA Modules:
  0.0 73.4 jit_solution(1137996255461645567)
XLA Ops:
  0.6 0.0 copy-start
  0.6 0.7 copy-done
  1.3 0.0 copy-start.1
  1.3 0.7 copy-done.1
  2.0 69.9 %shard_map.50 = (f32[4,8192]{1,0:T(4,128)S(1)}, f32[4,8192]{1,0:T(4,128)S(1)}, f32[2,4,256]{2,1,0:T(4,128)}, f32[10,4,128]{2,1,0:T(4,128)S(1)}) custom-call(f32[4,512]{1,0:T(4,128)S(1)} %copy-done, s32[2,32]{1,0:T(2,128)S(1)} %bitcast.1, bf16[32,2,256,256]{3,2,1,0:T(8,128)(2,1)} %tiles_hbm.1), custom_call_target="tpu_custom_call" | custom-call | tf_op jit(solution)/shard_map/pallas_call | solution.py:570
  71.9 0.6 slice_reduce_fusion
  72.6 0.8 %multiply_add_fusion = f32[4,8192]{1,0:T(4,128)} fusion(f32[4,8192]{1,0:T(4,128)S(1)} %get-tuple-element.7, f32[4,8192]{1,0:T(4,128)S(1)} %get-tuple-element.6, f32[4]{0:T(128)S(1)} %get-tuple-element.9, f32[4]{0:T(128)S(1)} %get-tuple-element.10, f32[4]{0:T(128)S(1)} %get-tuple-element.11, f32[4]{0:T(128)S(1)} %get-tuple-element.12, f32[4]{0:T(128)S(1)} %get-tuple-element.13), kind=kLoop, calls=%fused_computation.1 | loop fusion | flops 229376 | bytes 393296 | tf_op jit(solution)/shard_map/add | solution.py:593
Async XLA Ops:
  0.6 0.7 copy-start
  1.3 0.7 copy-start.1

commit v3 on v2

--- a/solution.py
+++ b/solution.py
@@ -13,10 +13,11 @@
 epsilon_sq = 1e-06
 
 MESH = pl.DeviceIdType.MESH
-COL_SUM = jnp.float32
+COL_SUMS = (jnp.float32, jnp.bfloat16)
 LOAD_PARTS = 8
 GROUP = 4
 HALVES = 2
+STEPS = 2
 
 
 def scope(name):
@@ -77,6 +78,8 @@
     half = tile_size // HALVES
     sides = observed_ref.shape[0]
     load_rows = row_tiles // LOAD_PARTS
+    step_tiles = own // STEPS
+    chunks = [(h, g) for h in range(HALVES) for g in range(STEPS)]
     flat = row_tiles * per_block
     key_rows = table_vec.shape[0] - per_block
     key_lanes = table_vec.shape[1]
@@ -164,11 +167,18 @@
         copy.start()
         copy.wait()
 
-    def last_term(c):
-        return table_ref[lax.div(c, key_lanes), lax.rem(c, key_lanes)]
+    def share_of(p):
+        return lax.div(p * own, key_lanes), lax.rem(p * own, key_lanes)
+
+    def last_term(share, i):
+        return table_ref[share[0], share[1] + i]
+
+    def place_of(c):
+        if own & (own - 1):
+            return lax.div(c, own), lax.rem(c, own)
+        return lax.shift_right_logical(c, own.bit_length() - 1), c & (own - 1)
 
     def turn_part(part):
-        load_part(part).wait()
         for j in range(load_rows):
             r = part * load_rows + j
             for h in range(HALVES):
@@ -211,48 +221,57 @@
             for k in range(per_block):
                 tile_loop(row_tiles, row_tiles, lambda r: chain(r, k))
         with scope(f"sendsums{turn}"):
-            for h in range(HALVES):
+            for n, (h, g) in enumerate(chunks):
                 for p in reversed(row_peers[1:]):
-                    for i in range(own):
-                        voxel_send[turn, h, p, i] = terms[h, last_term(p * own + i)].astype(bf16)
-                    if h == 0:
-                        voxel_send[turn, h, p, own] = high
-                        voxel_send[turn, h, p, own + 1] = low
-                    sums_copy(turn, h, p, p, me_row).start()
-        voxel_recv[turn, 0, me_row, own] = high
-        voxel_recv[turn, 0, me_row, own + 1] = low
-
-    def sums_copy(turn, h, peer, source, slot):
-        size = pl.ds(0, own + 2 if h == 0 else own)
+                    def fill(i, n=n, h=h, g=g, p=p, share=share_of(p)):
+                        term = terms[h, last_term(share, g * step_tiles + i)]
+                        voxel_send[turn, n, p, i] = term.astype(bf16)
+
+                    tile_loop(step_tiles, step_tiles, fill)
+                    if n == 0:
+                        voxel_send[turn, n, p, step_tiles] = high
+                        voxel_send[turn, n, p, step_tiles + 1] = low
+                    sums_copy(turn, n, p, p, me_row).start()
+        voxel_recv[turn, 0, me_row, step_tiles] = high
+        voxel_recv[turn, 0, me_row, step_tiles + 1] = low
+
+    def sums_size(n):
+        return pl.ds(0, step_tiles + 2 if n == 0 else step_tiles)
+
+    def sums_copy(turn, n, peer, source, slot):
         return copy_to(
-            "row", peer, voxel_send.at[turn, h, source, size], voxel_recv.at[turn, h, slot, size],
-            vs_send_sem.at[h], vs_recv_sem.at[h],
-        )
-
-    def voxel_copy(turn, h, peer, slot):
-        return copy_to(
-            "row", peer, voxel_panel[turn][h].at[slot], voxel_panel[turn][h].at[slot],
-            vp_send_sem.at[h], vp_recv_sem.at[h],
-        )
+            "row", peer, voxel_send.at[turn, n, source, sums_size(n)], voxel_recv.at[turn, n, slot, sums_size(n)],
+            vs_send_sem.at[n], vs_recv_sem.at[n],
+        )
+
+    def voxel_piece(n):
+        h, g = chunks[n]
+        return h, pl.ds(g * step_tiles, step_tiles + 2 if n == len(chunks) - 1 else step_tiles)
+
+    def voxel_copy(turn, n, peer, slot):
+        h, piece = voxel_piece(n)
+        ref = voxel_panel[turn][h].at[slot, piece]
+        return copy_to("row", peer, ref, ref, vp_send_sem.at[n], vp_recv_sem.at[n])
 
     def all_left(turn):
         whole = left_panel.at[turn, pl.ds(0, cols - 1)]
         return copy_to("col", col_peers[1], whole, whole, lp_send_sem, lp_recv_sem.at[0])
 
-    def all_sums(turn, h):
-        size = pl.ds(0, own + 2 if h == 0 else own)
+    def all_sums(turn, n):
+        others = pl.ds(0, rows - 1)
         return copy_to(
-            "row", row_peers[1], voxel_send.at[turn, h, pl.ds(0, rows - 1), size],
-            voxel_recv.at[turn, h, pl.ds(0, rows - 1), size], vs_send_sem.at[h], vs_recv_sem.at[h],
-        )
-
-    def all_voxels(turn, h):
-        whole = voxel_panel[turn][h].at[pl.ds(0, rows - 1)]
-        return copy_to("row", row_peers[1], whole, whole, vp_send_sem.at[h], vp_recv_sem.at[h])
+            "row", row_peers[1], voxel_send.at[turn, n, others, sums_size(n)],
+            voxel_recv.at[turn, n, others, sums_size(n)], vs_send_sem.at[n], vs_recv_sem.at[n],
+        )
+
+    def all_voxels(turn, n):
+        h, piece = voxel_piece(n)
+        whole = voxel_panel[turn][h].at[pl.ds(0, rows - 1), piece]
+        return copy_to("row", row_peers[1], whole, whole, vp_send_sem.at[n], vp_recv_sem.at[n])
 
     def all_rays(turn):
         return copy_to(
-            "col", col_peers[1], ray_send.at[turn, pl.ds(0, cols - 1)], ray_recv.at[turn, pl.ds(0, cols - 1)],
+            "col", col_peers[1], ray_send[turn].at[pl.ds(0, cols - 1)], ray_recv[turn].at[pl.ds(0, cols - 1)],
             rs_send_sem, rs_recv_sem,
         )
 
@@ -269,10 +288,12 @@
 
     def fill_low():
         for p in row_peers[1:]:
+            share = share_of(p)
             for h in range(HALVES):
                 for i in range(own):
-                    term = terms[h, last_term(p * own + i)]
-                    low_send[p, h, i] = (term - voxel_send[0, h, p, i].astype(f32)).astype(bf16)
+                    term = terms[h, last_term(share, i)]
+                    sent = voxel_send[0, h * STEPS + i // step_tiles, p, i % step_tiles]
+                    low_send[p, h, i] = (term - sent.astype(f32)).astype(bf16)
 
     low_groups = (row_peers[1:max(rows // 2, 1)], row_peers[max(rows // 2, 1):])
 
@@ -305,47 +326,51 @@
 
     def finish_right(turn, beta_of, alpha_before):
         beta = None
-        for h in range(HALVES):
-            with scope(f"waitsums{turn}{h}"):
-                all_sums(turn, h).wait_recv()
-            if h == 0:
+        my_share = share_of(me_row)
+        squares = jnp.zeros((sides, half), f32)
+        for n, (h, g) in enumerate(chunks):
+            with scope(f"waitsums{turn}{n}"):
+                all_sums(turn, n).wait_recv()
+            if n == 0:
                 beta, inverse, pull = beta_of()
-            with scope(f"right{turn}{h}"):
-                def one(i, squares, h=h):
-                    total = terms[h, last_term(me_row * own + i)]
+            with scope(f"right{turn}{n}"):
+                def one(i, squares, n=n, h=h, g=g):
+                    at = g * step_tiles + i
+                    total = terms[h, last_term(my_share, at)]
                     for p in row_peers[1:]:
-                        total = total + voxel_recv[turn, h, p, i].astype(f32)
-                    lanes = pl.ds(pl.multiple_of(i * tile_size + h * half, half), half)
+                        total = total + voxel_recv[turn, n, p, i].astype(f32)
+                    lanes = pl.ds(pl.multiple_of(at * tile_size + h * half, half), half)
                     right_raw = total * inverse
                     if turn > 0:
                         right_raw = right_raw - pull * right_refs[turn - 1][:, lanes]
                     right_refs[turn][:, lanes] = right_raw
-                    voxel_panel[turn][h][me_row, i] = right_raw.astype(bf16)
+                    voxel_panel[turn][h][me_row, at] = right_raw.astype(bf16)
                     return squares + right_raw * right_raw
 
                 def step(base, squares):
-                    for j in range(4):
-                        squares = one(base * 4 + j, squares)
+                    for j in range(min(4, step_tiles)):
+                        squares = one(base * min(4, step_tiles) + j, squares)
                     return squares
 
-                squares = lax.fori_loop(0, own // 4, step, jnp.zeros((sides, half), f32))
-                high, low = split(squares)
-                voxel_panel[turn][h][me_row, own] = high
-                voxel_panel[turn][h][me_row, own + 1] = low
+                squares = lax.fori_loop(0, step_tiles // min(4, step_tiles), step, squares)
+                if n == len(chunks) - 1:
+                    high, low = split(squares)
+                    voxel_panel[turn][h][me_row, own] = high
+                    voxel_panel[turn][h][me_row, own + 1] = low
                 for p in reversed(row_peers[1:]):
-                    voxel_copy(turn, h, p, me_row).start()
+                    voxel_copy(turn, n, p, me_row).start()
         return beta
 
     def beta_over_row(turn):
         total = jnp.zeros((sides, half), f32)
         for p in range(rows):
-            total = total + voxel_recv[turn, 0, p, own].astype(f32)
-            total = total + voxel_recv[turn, 0, p, own + 1].astype(f32)
+            total = total + voxel_recv[turn, 0, p, step_tiles].astype(f32)
+            total = total + voxel_recv[turn, 0, p, step_tiles + 1].astype(f32)
         return norm_of(total)
 
     def ray_copy(turn, peer, source, slot):
         return copy_to(
-            "col", peer, ray_send.at[turn, source], ray_recv.at[turn, slot],
+            "col", peer, ray_send[turn].at[source], ray_recv[turn].at[slot],
             rs_send_sem, rs_recv_sem,
         )
 
@@ -353,25 +378,41 @@
         pieces = []
         for k in range(per_block):
             c = cols_ref[k, r]
-            pieces.append(voxel_panel[turn][h][lax.div(c, own), lax.rem(c, own)])
+            pieces.append(voxel_panel[turn][h][place_of(c)])
         return jnp.concatenate(pieces, axis=1)
 
     def forward(turn):
         with scope(f"waitvox{turn}0"):
-            all_voxels(turn, 0).wait_recv()
+            for n in range(STEPS):
+                all_voxels(turn, n).wait_recv()
         with scope(f"f{turn}0"):
             def early(r):
                 ray_part[r] = jnp.dot(picked(turn, 0, r), turned[r, 0], preferred_element_type=f32)
 
             tile_loop(row_tiles, min(8, row_tiles), early)
         with scope(f"waitvox{turn}1"):
-            all_voxels(turn, 1).wait_recv()
+            for n in range(STEPS, len(chunks)):
+                all_voxels(turn, n).wait_recv()
         with scope(f"f{turn}1"):
             squares = jnp.zeros((sides, half), f32)
-            for h in range(HALVES):
-                for p in range(rows):
-                    squares = squares + voxel_panel[turn][h][p, own].astype(f32)
-                    squares = squares + voxel_panel[turn][h][p, own + 1].astype(f32)
+            for p in range(rows):
+                squares = squares + voxel_panel[turn][HALVES - 1][p, own].astype(f32)
+                squares = squares + voxel_panel[turn][HALVES - 1][p, own + 1].astype(f32)
+            kind = COL_SUMS[turn]
+
+            def put_squares(ref, p):
+                if kind == f32:
+                    ref[p, HALVES * rays] = squares
+                else:
+                    high, low = split(squares)
+                    ref[p, HALVES * rays] = high
+                    ref[p, HALVES * rays + 1] = low
+
+            def get_squares(p):
+                if kind == f32:
+                    return ray_recv[turn][p, HALVES * rays]
+                return ray_recv[turn][p, HALVES * rays].astype(f32) + ray_recv[turn][p, HALVES * rays + 1].astype(f32)
+
             farthest = col_peers[::-1]
             for start in range(0, cols, GROUP):
                 group = farthest[start:start + GROUP]
@@ -383,23 +424,23 @@
                         products.append((p, i, total))
                 for p, i, total in products:
                     for h in range(HALVES):
-                        ray_send[turn, p, HALVES * i + h] = total[:, h * half:(h + 1) * half]
+                        ray_send[turn][p, HALVES * i + h] = total[:, h * half:(h + 1) * half].astype(kind)
                 for p in group:
                     if p is not col_peers[0]:
-                        ray_send[turn, p, HALVES * rays] = squares
+                        put_squares(ray_send[turn], p)
                         ray_copy(turn, p, p, me_col).start()
             if turn == 0:
                 send_low(0)
-            ray_recv[turn, me_col, HALVES * rays] = squares
+            put_squares(ray_recv[turn], me_col)
         with scope(f"waitrays{turn}"):
-            pieces = [ray_send[turn, me_col, i] for i in range(HALVES * rays)]
+            pieces = [ray_send[turn][me_col, i].astype(f32) for i in range(HALVES * rays)]
             all_rays(turn).wait_recv()
             for p in col_peers[1:]:
                 for i in range(HALVES * rays):
-                    pieces[i] = pieces[i] + ray_recv[turn, p, i]
-            squares = ray_recv[turn, 0, HALVES * rays]
+                    pieces[i] = pieces[i] + ray_recv[turn][p, i].astype(f32)
+            squares = get_squares(0)
             for p in range(1, cols):
-                squares = squares + ray_recv[turn, p, HALVES * rays]
+                squares = squares + get_squares(p)
         sums = [jnp.concatenate(pieces[HALVES * i:HALVES * (i + 1)], axis=1) for i in range(rays)]
         return sums, norm_of(squares)
 
@@ -408,9 +449,9 @@
 
     def drain(turn):
         all_left(turn).wait_send()
-        for h in range(HALVES):
-            all_sums(turn, h).wait_send()
-            all_voxels(turn, h).wait_send()
+        for n in range(len(chunks)):
+            all_sums(turn, n).wait_send()
+            all_voxels(turn, n).wait_send()
         all_rays(turn).wait_send()
 
     publish_left(0, [side_tile(i) for i in range(rays)])
@@ -420,18 +461,22 @@
     with scope("table"):
         columns_load.wait()
         make_table()
+    for part in range(LOAD_PARTS):
+        load_part(part).wait()
+    adjoint(0)
     with scope("turn"):
-        for part in range(LOAD_PARTS):
+        for part in range(LOAD_PARTS // 2):
             turn_part(part)
-    adjoint(0)
-    with scope("fill"):
-        fill_low()
 
     def first_beta():
         beta = beta_over_row(0)
         return beta, 1.0 / beta, None
 
     beta0 = finish_right(0, first_beta, None)
+    with scope("turn2"):
+        for part in range(LOAD_PARTS // 2, LOAD_PARTS):
+            turn_part(part)
+        fill_low()
     sums, alpha0 = forward(0)
     alpha = wide(alpha0)
     beta = wide(beta0)
@@ -537,7 +582,11 @@
     share_len = own * tile_size
     dma = pltpu.SemaphoreType.DMA
     voxel_shape = (ITERS, HALVES, rows, own + 2, sides, half)
-    ray_shape = (ITERS, cols, HALVES * rays + 1, sides, half)
+    sums_shape = (ITERS, HALVES * STEPS, rows, own // STEPS + 2, sides, half)
+
+    def ray_shape(kind):
+        return (cols, HALVES * rays + (1 if kind == f32 else 2), sides, half)
+
     scratch = [
         pltpu.SMEM(tile_cols.shape[::-1], jnp.int32),
         pltpu.VMEM(tile_values.shape, bf16),
@@ -546,20 +595,20 @@
         pltpu.VMEM((row_tiles, sides, tile_size), f32),
         pltpu.VMEM((ITERS, cols, rays + 1, sides, tile_size), bf16),
         [[pltpu.VMEM(voxel_shape[2:], bf16) for _ in range(HALVES)] for _ in range(ITERS)],
-        pltpu.VMEM(voxel_shape, bf16),
-        pltpu.VMEM(voxel_shape, bf16),
+        pltpu.VMEM(sums_shape, bf16),
+        pltpu.VMEM(sums_shape, bf16),
         pltpu.VMEM((rows, HALVES, own, sides, half), bf16),
         pltpu.VMEM((rows, HALVES, own, sides, half), bf16),
-        pltpu.VMEM(ray_shape, COL_SUM),
-        pltpu.VMEM(ray_shape, COL_SUM),
+        [pltpu.VMEM(ray_shape(kind), kind) for kind in COL_SUMS],
+        [pltpu.VMEM(ray_shape(kind), kind) for kind in COL_SUMS],
         pltpu.VMEM((cols, sides, half), f32),
         pltpu.VMEM((2 * rows, sides, half), f32),
         pltpu.VMEM((key_rows + per_block, key_lanes), jnp.int32),
         pltpu.SMEM((key_rows + per_block, key_lanes), jnp.int32),
         dma, dma((LOAD_PARTS,)), dma,
         dma, dma((cols,)),
-        dma((HALVES,)), dma((HALVES,)),
-        dma((HALVES,)), dma((HALVES,)),
+        dma((HALVES * STEPS,)), dma((HALVES * STEPS,)),
+        dma((HALVES * STEPS,)), dma((HALVES * STEPS,)),
         dma((2,)), dma((2,)),
         dma, dma,
         dma, dma,

time: 73.5 us -> 72.2 us (0.982)
  Pallas kernels: 69.9 us -> 68.6 us
    pallas_call x1, Pallas kernels: 69.9 us -> 68.6 us  [local(): pl.pallas_call(functools.partial(solver_kernel, rows, cols, rays, own), o...]
where the time goes in v3:
time: 72.2 us; the launch traced here: 72 us
  Pallas kernels  68.6 us (95%)
  local copies, waits for them, and re-layouts  2 us (3%)
  other arithmetic  0.79 us (1%)
    pallas_call x1, Pallas kernels, local(): pl.pallas_call(functools.partial(solver_kernel, rows, cols, rays, own), o...  68.6 us

profile of v3, /device:TPU:1, one launch (start us, length us, event | category | flops | bytes accessed | tf_op | source)
XLA Modules:
  0.0 72.0 jit_solution(12797724245774849745)
XLA Ops:
  0.6 0.0 copy-start
  0.6 0.7 copy-done
  1.3 0.0 copy-start.1
  1.3 0.7 copy-done.1
  2.0 68.6 %shard_map.50 = (f32[4,8192]{1,0:T(4,128)S(1)}, f32[4,8192]{1,0:T(4,128)S(1)}, f32[2,4,256]{2,1,0:T(4,128)}, f32[10,4,128]{2,1,0:T(4,128)S(1)}) custom-call(f32[4,512]{1,0:T(4,128)S(1)} %copy-done, s32[2,32]{1,0:T(2,128)S(1)} %bitcast.1, bf16[32,2,256,256]{3,2,1,0:T(8,128)(2,1)} %tiles_hbm.1), custom_call_target="tpu_custom_call" | custom-call | tf_op jit(solution)/shard_map/pallas_call | solution.py:619
  70.6 0.6 slice_reduce_fusion
  71.2 0.8 %multiply_add_fusion = f32[4,8192]{1,0:T(4,128)} fusion(f32[4,8192]{1,0:T(4,128)S(1)} %get-tuple-element.7, f32[4,8192]{1,0:T(4,128)S(1)} %get-tuple-element.6, f32[4]{0:T(128)S(1)} %get-tuple-element.9, f32[4]{0:T(128)S(1)} %get-tuple-element.10, f32[4]{0:T(128)S(1)} %get-tuple-element.11, f32[4]{0:T(128)S(1)} %get-tuple-element.12, f32[4]{0:T(128)S(1)} %get-tuple-element.13), kind=kLoop, calls=%fused_computation.1 | loop fusion | flops 229376 | bytes 393296 | tf_op jit(solution)/shard_map/add | solution.py:642
Async XLA Ops:
  0.6 0.7 copy-start
  1.3 0.7 copy-start.1

commit v4 on v3

--- a/solution.py
+++ b/solution.py
@@ -15,8 +15,9 @@
 MESH = pl.DeviceIdType.MESH
 COL_SUMS = (jnp.float32, jnp.bfloat16)
 LOAD_PARTS = 8
-GROUP = 4
+GROUP = 8
 HALVES = 2
+CHAIN = 4
 STEPS = 2
 
 
@@ -213,13 +214,21 @@
             for h in range(HALVES):
                 terms[h, 0] = jnp.zeros((sides, half), f32)
 
-            def chain(r, k):
-                before = table_ref[key_rows + k, r]
+            def chain(start, k):
+                slots = [1 + k * row_tiles + start + j for j in range(CHAIN)]
+                before = [table_ref[key_rows + k, start + j] for j in range(CHAIN)]
+                outside = [jnp.where(b >= slots[0], 0, b) for b in before]
                 for h in range(HALVES):
-                    terms[h, 1 + k * row_tiles + r] = terms[h, 1 + k * row_tiles + r] + terms[h, before]
+                    sums = [terms[h, slots[j]] + terms[h, outside[j]] for j in range(CHAIN)]
+                    for j in range(1, CHAIN):
+                        for i in range(j):
+                            sums[j] = sums[j] + jnp.where(before[j] == slots[i], sums[i], jnp.zeros_like(sums[i]))
+                    for j in range(CHAIN):
+                        terms[h, slots[j]] = sums[j]
 
             for k in range(per_block):
-                tile_loop(row_tiles, row_tiles, lambda r: chain(r, k))
+                for start in range(0, row_tiles, CHAIN):
+                    chain(start, k)
         with scope(f"sendsums{turn}"):
             for n, (h, g) in enumerate(chunks):
                 for p in reversed(row_peers[1:]):
@@ -526,10 +535,12 @@
             device_id={"row": peer[0], "col": peer[1]}, device_id_type=MESH,
         )
 
-    def all_sum(ref, peers, me, value, send_sem, recv_sem):
+    def start_sum(ref, peers, me, value, send_sem, recv_sem):
         ref[me] = value
         for peer in reversed(peers):
             norm_copy(ref, peer, me, send_sem, recv_sem).start()
+
+    def end_sum(ref, peers, send_sem, recv_sem):
         norm_copy(ref, peers[0], pl.ds(0, len(peers)), send_sem, recv_sem).wait()
         total = ref[0]
         for p in range(1, len(peers) + 1):
@@ -537,13 +548,16 @@
         return total
 
     squares = fold(sum_of_squares(left_raw))
-    send_low(1)
     with scope("normcol"):
-        squares = all_sum(norm_col, place_peers, my_place, squares, nc_send_sem, nc_recv_sem)
+        start_sum(norm_col, place_peers, my_place, squares, nc_send_sem, nc_recv_sem)
+        send_low(1)
+        squares = end_sum(norm_col, place_peers, nc_send_sem, nc_recv_sem)
     with scope("normrow"):
-        squares = all_sum(norm_row, part_peers, my_part * rows + me_row, squares, nr_send_sem, nr_recv_sem)
+        start_sum(norm_row, part_peers, my_part * rows + me_row, squares, nr_send_sem, nr_recv_sem)
     with scope("addlow2"):
         add_low(1, 1.0 / beta0, beta1 / alpha0)
+    with scope("normrow2"):
+        squares = end_sum(norm_row, part_peers, nr_send_sem, nr_recv_sem)
     beta2 = norm_of(squares)
     rho2 = jnp.sqrt(rhobar1 * rhobar1 + beta2 * beta2)
     cosine2 = rhobar1 / rho2

time: 72.2 us -> 71.6 us (level)
  no operation moved by 1% of the time
where the time goes in v4:
time: 71.6 us; the launch traced here: 71.4 us
  Pallas kernels  68 us (95%)
  local copies, waits for them, and re-layouts  2 us (3%)
  other arithmetic  0.79 us (1%)
    pallas_call x1, Pallas kernels, local(): pl.pallas_call(functools.partial(solver_kernel, rows, cols, rays, own), o...  68 us

profile of v4, /device:TPU:1, one launch (start us, length us, event | category | flops | bytes accessed | tf_op | source)
XLA Modules:
  0.0 71.4 jit_solution(6625722195860140011)
XLA Ops:
  0.6 0.0 copy-start
  0.6 0.7 copy-done
  1.3 0.0 copy-start.1
  1.3 0.7 copy-done.1
  2.0 68.0 %shard_map.50 = (f32[4,8192]{1,0:T(4,128)S(1)}, f32[4,8192]{1,0:T(4,128)S(1)}, f32[2,4,256]{2,1,0:T(4,128)}, f32[10,4,128]{2,1,0:T(4,128)S(1)}) custom-call(f32[4,512]{1,0:T(4,128)S(1)} %copy-done, s32[2,32]{1,0:T(2,128)S(1)} %bitcast.1, bf16[32,2,256,256]{3,2,1,0:T(8,128)(2,1)} %tiles_hbm.1), custom_call_target="tpu_custom_call" | custom-call | tf_op jit(solution)/shard_map/pallas_call | solution.py:633
  70.0 0.6 slice_reduce_fusion
  70.6 0.8 %multiply_add_fusion = f32[4,8192]{1,0:T(4,128)} fusion(f32[4,8192]{1,0:T(4,128)S(1)} %get-tuple-element.7, f32[4,8192]{1,0:T(4,128)S(1)} %get-tuple-element.6, f32[4]{0:T(128)S(1)} %get-tuple-element.9, f32[4]{0:T(128)S(1)} %get-tuple-element.10, f32[4]{0:T(128)S(1)} %get-tuple-element.11, f32[4]{0:T(128)S(1)} %get-tuple-element.12, f32[4]{0:T(128)S(1)} %get-tuple-element.13), kind=kLoop, calls=%fused_computation.1 | loop fusion | flops 229376 | bytes 393296 | tf_op jit(solution)/shard_map/add | solution.py:656
Async XLA Ops:
  0.6 0.7 copy-start
  1.3 0.7 copy-start.1
